TPU v7x, 512 devices: a whole 4x8x8 slice. The times are simulated.
512 devices in a mesh: row: 16 (over y, core), col: 32 (over z, x).
Axes of the slice: x: 4, y: 8, z: 8, core: 2. Of those that a mesh axis runs over, the one named last changes fastest.
Arguments:
- particles: float32 [16384, 128], P('row'), may hold values from -4 to 4
- log_weights: float32 [16384], P('row'), may hold values from -8 to 8
- targets: float32 [49152, 128], P('col'), may hold values from -5 to 5
Outputs:
- new_particles: float32 [49152, 128], P(('col', 'row'))
All inputs are finite; a program needn't handle non-finite values.
Results may differ from a plain program's by a relative error of at most 0.005.
Values sent between devices are 32-bit elements; how exact they have to be, the bound alone decides.
No kernel may reach another device: no remote copies, remote signals or barrier semaphores. Data moves between devices by JAX's collectives and lax.ppermute only.
A program may use at most 64 MiB of HBM per device.

v0:
```python
import math
import jax
import jax.numpy as jnp
from jax import lax
from jax.sharding import PartitionSpec as P

ITERS = 3
EPS = 0.01


def cost_tile(source, points):
    source_sq = jnp.sum(source * source, axis=1)
    points_sq = jnp.sum(points * points, axis=1)
    cross = jnp.dot(
        source, points.T, precision=lax.Precision.HIGHEST, preferred_element_type=jnp.float32
    )
    return (source_sq[:, None] + points_sq[None, :] - 2.0 * cross) / source.shape[1]


def row_update(particles, log_weights, targets, col_pot, block_count, block_rows):
    maxima = []
    totals = []
    for index in range(block_count):
        source = particles[index * block_rows : (index + 1) * block_rows]
        scores = (col_pot[None, :] - cost_tile(source, targets)) / EPS
        top = jnp.max(scores, axis=1)
        maxima.append(top)
        totals.append(jnp.sum(jnp.exp(scores - top[:, None]), axis=1))
    local_top = jnp.concatenate(maxima)
    local_sum = jnp.concatenate(totals)
    top = lax.pmax(local_top, "col")
    summed = lax.psum(local_sum * jnp.exp(local_top - top), "col")
    return EPS * (log_weights - (top + jnp.log(summed)))


def col_update(particles, targets, row_pot, block_count, block_rows):
    width = targets.shape[0]
    top = jnp.full((width,), -1e30, jnp.float32)
    summed = jnp.zeros((width,), jnp.float32)
    for index in range(block_count):
        source = particles[index * block_rows : (index + 1) * block_rows]
        potential = row_pot[index * block_rows : (index + 1) * block_rows]
        scores = (potential[:, None] - cost_tile(source, targets)) / EPS
        fresh = jnp.maximum(top, jnp.max(scores, axis=0))
        summed = summed * jnp.exp(top - fresh) + jnp.sum(jnp.exp(scores - fresh[None, :]), axis=0)
        top = fresh
    global_top = lax.pmax(top, "row")
    summed = lax.psum(summed * jnp.exp(top - global_top), "row")
    top = global_top
    return top + jnp.log(summed)


def per_device(particles, log_weights, targets):
    row_count = particles.shape[0]
    block_count = max(1, row_count // 512)
    block_rows = row_count // block_count
    log_count = math.log(targets.shape[0] * lax.axis_size("col"))
    col_pot = jnp.zeros((targets.shape[0],), jnp.float32)
    col_lse = col_pot
    row_pot = log_weights
    for iteration in range(ITERS):
        row_pot = row_update(particles, log_weights, targets, col_pot, block_count, block_rows)
        col_lse = col_update(particles, targets, row_pot, block_count, block_rows)
        col_pot = EPS * (-log_count - col_lse)
    particles_half = particles.astype(jnp.bfloat16)
    acc = jnp.zeros(
        (lax.axis_size("row") * (targets.shape[0] // lax.axis_size("row")), particles.shape[1]),
        jnp.float32,
    )
    for index in range(block_count):
        source = particles[index * block_rows : (index + 1) * block_rows]
        potential = row_pot[index * block_rows : (index + 1) * block_rows]
        plan = jnp.exp(
            (potential[:, None] - cost_tile(source, targets)) / EPS - col_lse[None, :]
        ).astype(jnp.bfloat16)
        source_half = particles_half[index * block_rows : (index + 1) * block_rows]
        acc = acc + lax.dot_general(
            plan, source_half, (((0,), (0,)), ((), ())), preferred_element_type=jnp.float32
        )
    return lax.psum_scatter(acc, "row", scatter_dimension=0, tiled=True)


def solution(mesh):
    placed = (P("row", None), P("row"), P("col", None))
    return jax.shard_map(
        per_device, mesh=mesh, in_specs=placed, out_specs=P(("col", "row"), None), check_vma=False
    )
```

profile of v0, /device:TPU:25, one launch (start us, length us, event | category | flops | bytes accessed | tf_op | source)
XLA Modules:
  0.0 693.4 jit_solution(18334036911586414496)
XLA Ops:
  10.4 4.5 fusion.5
  14.9 4.8 fusion.4
  19.8 66.7 %pmax.42 = f32[1024]{0:T(1024)S(1)} all-reduce(f32[1024]{0:T(1024)S(1)} %pad_maximum_fusion), channel_id=1, replica_groups=mesh['row'=16,'col'=32] {'col'}, use_global_device_ids=true, to_apply=%region_5.0 | all-reduce | flops 1024 | bytes 8192 | tf_op jit(solution)/shard_map/pmax | solution.py:31
  86.4 3.2 exponential_reduce_fusion.10
  89.7 56.1 %psum.42 = f32[1024]{0:T(1024)S(1)} all-reduce(f32[1024]{0:T(1024)S(1)} %maximum_multiply_fusion), channel_id=1, replica_groups=mesh['row'=16,'col'=32] {'col'}, use_global_device_ids=true, to_apply=%region_8.0 | all-reduce | flops 1024 | bytes 8192 | tf_op jit(solution)/shard_map/psum | solution.py:32
  145.8 2.3 fusion.6
  149.2 51.3 %pmax.43 = f32[1536]{0:T(1024)S(1)} all-reduce(f32[1536]{0:T(1024)S(1)} %get-tuple-element.16), channel_id=1, replica_groups=mesh['row'=16,'col'=32] {'row'}, use_global_device_ids=true, to_apply=%region_11.0 | all-reduce | flops 1536 | bytes 12288 | tf_op jit(solution)/shard_map/pmax | solution.py:47
  200.5 2.6 exponential_reduce_fusion.9
  203.2 24.2 %psum.43 = f32[1536]{0:T(1024)S(1)} all-reduce(f32[1536]{0:T(1024)S(1)} %exponential_multiply_fusion.2), channel_id=1, replica_groups=mesh['row'=16,'col'=32] {'row'}, use_global_device_ids=true, to_apply=%region_14.0 | all-reduce | flops 1536 | bytes 12288 | tf_op jit(solution)/shard_map/psum | solution.py:48
  227.4 2.4 fusion.8
  232.0 57.4 %pmax.44 = f32[1024]{0:T(1024)S(1)} all-reduce(f32[1024]{0:T(1024)S(1)} %pad_maximum_fusion.1), channel_id=1, replica_groups=mesh['row'=16,'col'=32] {'col'}, use_global_device_ids=true, to_apply=%region_17.0 | all-reduce | flops 1024 | bytes 8192 | tf_op jit(solution)/shard_map/pmax | solution.py:31
  289.5 56.2 %psum.44 = f32[1024]{0:T(1024)S(1)} all-reduce(f32[1024]{0:T(1024)S(1)} %maximum_multiply_fusion.1), channel_id=1, replica_groups=mesh['row'=16,'col'=32] {'col'}, use_global_device_ids=true, to_apply=%region_20.0 | all-reduce | flops 1024 | bytes 8192 | tf_op jit(solution)/shard_map/psum | solution.py:32
  345.7 2.3 fusion.10
  349.1 51.7 %pmax.45 = f32[1536]{0:T(1024)S(1)} all-reduce(f32[1536]{0:T(1024)S(1)} %get-tuple-element.14), channel_id=1, replica_groups=mesh['row'=16,'col'=32] {'row'}, use_global_device_ids=true, to_apply=%region_23.0 | all-reduce | flops 1536 | bytes 12288 | tf_op jit(solution)/shard_map/pmax | solution.py:47
  400.8 2.6 exponential_reduce_fusion.5
  403.4 24.1 %psum.45 = f32[1536]{0:T(1024)S(1)} all-reduce(f32[1536]{0:T(1024)S(1)} %exponential_multiply_fusion.1), channel_id=1, replica_groups=mesh['row'=16,'col'=32] {'row'}, use_global_device_ids=true, to_apply=%region_26.0 | all-reduce | flops 1536 | bytes 12288 | tf_op jit(solution)/shard_map/psum | solution.py:48
  427.5 2.4 fusion.12
  432.1 57.4 %pmax.46 = f32[1024]{0:T(1024)S(1)} all-reduce(f32[1024]{0:T(1024)S(1)} %pad_maximum_fusion.2), channel_id=1, replica_groups=mesh['row'=16,'col'=32] {'col'}, use_global_device_ids=true, to_apply=%region_29.0 | all-reduce | flops 1024 | bytes 8192 | tf_op jit(solution)/shard_map/pmax | solution.py:31
  489.5 56.2 %psum.46 = f32[1024]{0:T(1024)S(1)} all-reduce(f32[1024]{0:T(1024)S(1)} %maximum_multiply_fusion.2), channel_id=1, replica_groups=mesh['row'=16,'col'=32] {'col'}, use_global_device_ids=true, to_apply=%region_32.0 | all-reduce | flops 1024 | bytes 8192 | tf_op jit(solution)/shard_map/psum | solution.py:32
  545.7 2.3 fusion.14
  548.4 51.7 %pmax.47 = f32[1536]{0:T(1024)S(1)} all-reduce(f32[1536]{0:T(1024)S(1)} %get-tuple-element.12), channel_id=1, replica_groups=mesh['row'=16,'col'=32] {'row'}, use_global_device_ids=true, to_apply=%region_35.0 | all-reduce | flops 1536 | bytes 12288 | tf_op jit(solution)/shard_map/pmax | solution.py:47
  602.8 24.1 %psum.47 = f32[1536]{0:T(1024)S(1)} all-reduce(f32[1536]{0:T(1024)S(1)} %exponential_multiply_fusion), channel_id=1, replica_groups=mesh['row'=16,'col'=32] {'row'}, use_global_device_ids=true, to_apply=%region_38.0 | all-reduce | flops 1536 | bytes 12288 | tf_op jit(solution)/shard_map/psum | solution.py:48
  626.9 2.7 fusion.16
  631.4 55.2 %reduce-scatter.2.cloned.1.call-done = f32[96,128]{1,0:T(8,128)} async-done(((f32[1536,128]{1,0:T(8,128)}), f32[96,128]{1,0:T(8,128)}) %reduce-scatter.2.cloned.1.call-update) | async-done | bytes 49168 | tf_op jit(solution)/shard_map/reduce_scatter | solution.py:80
  (50 shorter events, 15.2 us)
Async XLA Ops:
  6.5 680.0 %reduce-scatter.2.cloned.1.call-start = ((), (), s32[]{:S(2)}) async-start(), calls=%async_computation.1 | async-start | bytes 835584 | tf_op jit(solution)/shard_map/reduce_scatter | solution.py:80
  8.9 6.0 copy-start.3
  8.9 6.0 copy-start.4
  86.4 59.4 %copy-start.5 = (f32[1024]{0:T(1024)S(1)}, f32[1024]{0:T(1024)}, u32[]{:S(2)}) copy-start(f32[1024]{0:T(1024)} %param.4) | copy-start | bytes 12292
  227.4 2.8 copy-start
  427.5 2.8 copy-start.1
  600.2 1.9 copy-start.2
Sparse Core Ops, SparseCore 0:
  631.5 54.9 reduce-scatter.1
where the time goes:
time: 694 us; the launch traced here: 693 us
  blocking collectives  577 us (83%)
  waiting for transfers between devices  55.2 us (8%)
  other arithmetic  31.5 us (5%)
  matrix products  13.8 us (2%)
  between operations  13.7 us (2%)
    pmax x3, blocking collectives, row_update(): top = lax.pmax(local_top, 'col')  182 us
    psum x3, blocking collectives, row_update(): summed = lax.psum(local_sum * jnp.exp(local_top - top), 'col')  168 us
    pmax x3, blocking collectives, col_update(): global_top = lax.pmax(top, 'row')  155 us
    psum x3, blocking collectives, col_update(): summed = lax.psum(summed * jnp.exp(top - global_top), 'row')  72.4 us
    reduce_scatter x1, waiting for transfers between devices, per_device(): return lax.psum_scatter(acc, 'row', scatter_dimension=0, tiled=True)  55.2 us
  transfers between devices with their start and end apart: 1, of which 1 were waited for; matrix products, arithmetic and copies ran while one was open for 0% of the time, Pallas kernels for 0%

commit v1 on v0

--- a/solution.py
+++ b/solution.py
@@ -45,7 +45,7 @@
         summed = summed * jnp.exp(top - fresh) + jnp.sum(jnp.exp(scores - fresh[None, :]), axis=0)
         top = fresh
     global_top = lax.pmax(top, "row")
-    summed = lax.psum(summed * jnp.exp(top - global_top), "row")
+    summed = lax.all_gather(summed * jnp.exp(top - global_top), "row").sum(axis=0)
     top = global_top
     return top + jnp.log(summed)
 

time: 694 us -> 666 us (0.960)
  the two profiles are of different devices: /device:TPU:25 before, /device:TPU:29 now
where the time goes in v1:
time: 666 us; the launch traced here: 665 us
  blocking collectives  546 us (82%)
  waiting for transfers between devices  57.5 us (9%)
  other arithmetic  31.7 us (5%)
  matrix products  13.8 us (2%)
  between operations  13.7 us (2%)
    pmax x3, blocking collectives, row_update(): top = lax.pmax(local_top, 'col')  178 us
    psum x3, blocking collectives, row_update(): summed = lax.psum(local_sum * jnp.exp(local_top - top), 'col')  169 us
    pmax x3, blocking collectives, col_update(): global_top = lax.pmax(top, 'row')  149 us
    reduce_scatter x1, waiting for transfers between devices, per_device(): return lax.psum_scatter(acc, 'row', scatter_dimension=0, tiled=True)  57.5 us
    all_gather x3, blocking collectives, col_update(): lax.all_gather(summed * jnp.exp(top - global_top), 'row').sum(axis=0)  50.9 us
  transfers between devices with their start and end apart: 1, of which 1 were waited for; matrix products, arithmetic and copies ran while one was open for 0% of the time, Pallas kernels for 0%

profile of v1, /device:TPU:29, one launch (start us, length us, event | category | flops | bytes accessed | tf_op | source)
XLA Modules:
  0.0 665.2 jit_solution(1512242927766748921)
XLA Ops:
  10.4 4.5 fusion.5
  14.9 4.8 fusion.4
  19.8 62.4 %pmax.42 = f32[1024]{0:T(1024)S(1)} all-reduce(f32[1024]{0:T(1024)S(1)} %pad_maximum_fusion), channel_id=1, replica_groups=mesh['row'=16,'col'=32] {'col'}, use_global_device_ids=true, to_apply=%region_5.0 | all-reduce | flops 1024 | bytes 8192 | tf_op jit(solution)/shard_map/pmax | solution.py:31
  82.1 3.2 exponential_reduce_fusion.10
  85.4 56.1 %psum.21 = f32[1024]{0:T(1024)S(1)} all-reduce(f32[1024]{0:T(1024)S(1)} %maximum_multiply_fusion), channel_id=1, replica_groups=mesh['row'=16,'col'=32] {'col'}, use_global_device_ids=true, to_apply=%region_8.0 | all-reduce | flops 1024 | bytes 8192 | tf_op jit(solution)/shard_map/psum | solution.py:32
  141.5 2.3 fusion.6
  144.9 51.3 %pmax.43 = f32[1536]{0:T(1024)S(1)} all-reduce(f32[1536]{0:T(1024)S(1)} %get-tuple-element.16), channel_id=1, replica_groups=mesh['row'=16,'col'=32] {'row'}, use_global_device_ids=true, to_apply=%region_11.0 | all-reduce | flops 1536 | bytes 12288 | tf_op jit(solution)/shard_map/pmax | solution.py:47
  196.3 2.6 exponential_reduce_fusion.9
  198.9 17.1 %all-gather.3 = f32[16,1,1536]{2,1,0:T(1,128)S(1)} all-gather(f32[1,1,1536]{2,1,0:T(1,128)S(1)} %reshape.45), channel_id=2, replica_groups=mesh['row'=16,'col'=32] {'row'}, dimensions={0}, use_global_device_ids=true | all-gather | bytes 104448 | tf_op jit(solution)/shard_map/all_gather | solution.py:48
  216.1 2.4 fusion.8
  220.7 57.7 %pmax.44 = f32[1024]{0:T(1024)S(1)} all-reduce(f32[1024]{0:T(1024)S(1)} %pad_maximum_fusion.1), channel_id=1, replica_groups=mesh['row'=16,'col'=32] {'col'}, use_global_device_ids=true, to_apply=%region_17.0 | all-reduce | flops 1024 | bytes 8192 | tf_op jit(solution)/shard_map/pmax | solution.py:31
  278.3 56.3 %psum.22 = f32[1024]{0:T(1024)S(1)} all-reduce(f32[1024]{0:T(1024)S(1)} %maximum_multiply_fusion.1), channel_id=1, replica_groups=mesh['row'=16,'col'=32] {'col'}, use_global_device_ids=true, to_apply=%region_20.0 | all-reduce | flops 1024 | bytes 8192 | tf_op jit(solution)/shard_map/psum | solution.py:32
  334.6 2.3 fusion.10
  338.0 48.9 %pmax.45 = f32[1536]{0:T(1024)S(1)} all-reduce(f32[1536]{0:T(1024)S(1)} %get-tuple-element.14), channel_id=1, replica_groups=mesh['row'=16,'col'=32] {'row'}, use_global_device_ids=true, to_apply=%region_23.0 | all-reduce | flops 1536 | bytes 12288 | tf_op jit(solution)/shard_map/pmax | solution.py:47
  386.9 2.6 exponential_reduce_fusion.5
  389.6 16.9 %all-gather.4 = f32[16,1,1536]{2,1,0:T(1,128)S(1)} all-gather(f32[1,1,1536]{2,1,0:T(1,128)S(1)} %reshape.47), channel_id=3, replica_groups=mesh['row'=16,'col'=32] {'row'}, dimensions={0}, use_global_device_ids=true | all-gather | bytes 104448 | tf_op jit(solution)/shard_map/all_gather | solution.py:48
  406.6 2.4 fusion.12
  411.1 57.7 %pmax.46 = f32[1024]{0:T(1024)S(1)} all-reduce(f32[1024]{0:T(1024)S(1)} %pad_maximum_fusion.2), channel_id=1, replica_groups=mesh['row'=16,'col'=32] {'col'}, use_global_device_ids=true, to_apply=%region_29.0 | all-reduce | flops 1024 | bytes 8192 | tf_op jit(solution)/shard_map/pmax | solution.py:31
  468.9 56.2 %psum.23 = f32[1024]{0:T(1024)S(1)} all-reduce(f32[1024]{0:T(1024)S(1)} %maximum_multiply_fusion.2), channel_id=1, replica_groups=mesh['row'=16,'col'=32] {'col'}, use_global_device_ids=true, to_apply=%region_32.0 | all-reduce | flops 1024 | bytes 8192 | tf_op jit(solution)/shard_map/psum | solution.py:32
  525.1 2.3 fusion.14
  527.8 48.9 %pmax.47 = f32[1536]{0:T(1024)S(1)} all-reduce(f32[1536]{0:T(1024)S(1)} %get-tuple-element.12), channel_id=1, replica_groups=mesh['row'=16,'col'=32] {'row'}, use_global_device_ids=true, to_apply=%region_35.0 | all-reduce | flops 1536 | bytes 12288 | tf_op jit(solution)/shard_map/pmax | solution.py:47
  579.4 16.9 %all-gather.5 = f32[16,1,1536]{2,1,0:T(1,128)S(1)} all-gather(f32[1,1,1536]{2,1,0:T(1,128)S(1)} %reshape.49), channel_id=4, replica_groups=mesh['row'=16,'col'=32] {'row'}, dimensions={0}, use_global_device_ids=true | all-gather | bytes 104448 | tf_op jit(solution)/shard_map/all_gather | solution.py:48
  596.4 2.7 fusion.16
  600.9 57.5 %reduce-scatter.2.cloned.1.call-done = f32[96,128]{1,0:T(8,128)} async-done(((f32[1536,128]{1,0:T(8,128)}), f32[96,128]{1,0:T(8,128)}) %reduce-scatter.2.cloned.1.call-update) | async-done | bytes 49168 | tf_op jit(solution)/shard_map/reduce_scatter | solution.py:80
  (56 shorter events, 15.4 us)
Async XLA Ops:
  6.5 651.8 %reduce-scatter.2.cloned.1.call-start = ((), (), s32[]{:S(2)}) async-start(), calls=%async_computation.1 | async-start | bytes 835584 | tf_op jit(solution)/shard_map/reduce_scatter | solution.py:80
  8.9 6.0 copy-start.3
  8.9 6.0 copy-start.4
  82.1 59.4 %copy-start.5 = (f32[1024]{0:T(1024)S(1)}, f32[1024]{0:T(1024)}, u32[]{:S(2)}) copy-start(f32[1024]{0:T(1024)} %param.4) | copy-start | bytes 12292
  216.0 2.8 copy-start
  406.5 2.8 copy-start.1
  576.8 1.9 copy-start.2
Sparse Core Ops, SparseCore 0:
  601.0 57.2 reduce-scatter.1
